TPU v7x, 32 devices: a whole 2x2x4 slice. The times are simulated.
32 devices in a mesh: wave: 8 (over z, y), lev: 4 (over x, core).
Axes of the slice: x: 2, y: 2, z: 4, core: 2. Of those that a mesh axis runs over, the one named last changes fastest.
Arguments:
- spectral: float32 [8, 136, 2, 1280], P('wave', 'lev'), may hold values from -6 to 6
- to_modes: float32 [136, 136], replicated
- from_modes: float32 [136, 136], replicated
- mode_depths: float32 [136], replicated, may hold values from 0.05 to 5
- legendre: float32 [8, 16, 1280], P('wave'), may hold values from -0.03125 to 0.03125
- wave_ids: int32 [8], replicated, may hold values from 0 to 1279, as said below
- lat_points: int32 [16], P('wave'), may hold values from 20 to 5136, as said below
Outputs:
- grid: float32 [136, 16, 5136], P('lev', 'wave')
Inputs may be any that keep to these rules, and one draw needn't show every extreme that they name: `wave_ids`: distinct and ascending; 0 and 1279 are always among them. `lat_points`: each is 20 + 4 k for a whole k; not falling along the latitudes; the last is always 5136.
All inputs are finite; a program needn't handle non-finite values.
Results may differ from a plain program's by a relative error of at most 0.0003.
Values sent between devices are 32-bit elements; how exact they have to be, the bound alone decides.
No kernel may reach another device: no remote copies, remote signals or barrier semaphores. Data moves between devices by JAX's collectives and lax.ppermute only.
A program may use at most 64 MiB of HBM per device.

v0:
```python
import math
import jax
import jax.numpy as jnp
from jax import lax
from jax.sharding import PartitionSpec as P

LONS = 5136
two_pi = 2.0 * math.pi


def on_device(spectral, to_modes, from_modes, mode_depths, legendre, wave_ids, lat_points):
    highest = lax.Precision.HIGHEST
    waves_here = spectral.shape[0]
    total_orders = spectral.shape[3]
    block_len = total_orders // lax.axis_size("lev")
    columns = lax.all_to_all(spectral, "lev", split_axis=3, concat_axis=1, tiled=True)
    mode_coeffs = jnp.einsum("kl,wlcn->wkcn", to_modes, columns, precision=highest)
    first_order = lax.axis_index("lev") * block_len
    order_ids = first_order + jnp.arange(block_len)
    orders = order_ids.astype(jnp.float32)
    damping = 1.0 + mode_depths[:, None] * (orders * (orders + 1.0))[None, :] / float(
        total_orders * total_orders
    )
    divergence = jnp.einsum(
        "lk,wkcn->wlcn", from_modes, mode_coeffs / damping[None, :, None, :], precision=highest
    )
    own_ids = lax.dynamic_slice_in_dim(wave_ids, lax.axis_index("wave") * waves_here, waves_here)
    level_major = lax.all_to_all(divergence, "lev", split_axis=1, concat_axis=3, tiled=True)
    keep_mask = (jnp.arange(total_orders)[None, :] >= own_ids[:, None]).astype(jnp.float32)
    fourier = jnp.einsum(
        "wjn,wlcn->lwcj", legendre * keep_mask[:, None, :], level_major, precision=highest
    )
    band_data = lax.all_to_all(fourier, "wave", split_axis=3, concat_axis=1, tiled=True)
    positions = jnp.arange(LONS)

    def one_row(inputs):
        coeffs, points = inputs
        residue = wave_ids[:, None] * positions[None, :] % points
        phases = jnp.float32(two_pi) * residue.astype(jnp.float32) / points.astype(jnp.float32)
        weight = jnp.where(2 * wave_ids < points, jnp.where(wave_ids == 0, 1.0, 2.0), 0.0).astype(
            jnp.float32
        )
        basis_table = jnp.concatenate(
            [jnp.cos(phases) * weight[:, None], jnp.sin(phases) * weight[:, None]], 0
        )
        coefficient = jnp.concatenate([coeffs[:, :, 0], -coeffs[:, :, 1]], 1)
        lat_row = jnp.dot(coefficient, basis_table, precision=highest)
        return lat_row * (positions < points).astype(jnp.float32)[None, :]

    lat_rows = lax.map(one_row, (jnp.moveaxis(band_data, 3, 0), lat_points))
    return jnp.transpose(lat_rows, (1, 0, 2))


def solution(mesh):
    return jax.shard_map(
        on_device,
        mesh=mesh,
        in_specs=(
            P("wave", "lev", None, None),
            P(),
            P(),
            P(),
            P("wave", None, None),
            P(),
            P("wave"),
        ),
        out_specs=P("lev", "wave", None),
        check_vma=False,
    )
```

profile of v0, /device:TPU:0, one launch (start us, length us, event | category | flops | bytes accessed | tf_op | source)
XLA Modules:
  0.0 79.2 jit_solution(634367973494513038)
XLA Ops:
  0.0 2.6 %copy.29 = f32[1,34,2,1280]{1,2,0,3:T(2,128)S(1)} copy(f32[1,34,2,1280]{3,2,1,0:T(2,128)} %param.9) | data formatting | bytes 696320 | tf_op args[0]
  2.7 3.0 %reshape.90 = f32[4,1,21760]{2,1,0:T(1,128)} reshape(f32[1280,1,2,34]{3,2,1,0:T(2,128)S(1)} %bitcast.71) | data formatting | bytes 696320
  5.7 4.2 %all-to-all-start = ((f32[4,1,21760]{2,1,0:T(1,128)}), f32[4,1,21760]{2,1,0:T(1,128)S(1)}, u32[]{:S(2)}, u32[]{:S(2)}) async-start(f32[4,1,21760]{2,1,0:T(1,128)} %reshape.90), calls=%async_computation | async-start | bytes 696320 | tf_op jit(solution)/shard_map/all_to_all | solution.py:16
  10.0 6.9 %all-to-all-done = f32[4,1,21760]{2,1,0:T(1,128)S(1)} async-done(((f32[4,1,21760]{2,1,0:T(1,128)}), f32[4,1,21760]{2,1,0:T(1,128)S(1)}, u32[]{:S(2)}, u32[]{:S(2)}) %all-to-all-start) | async-done | bytes 348192 | tf_op jit(solution)/shard_map/all_to_all | solution.py:16
  17.4 1.6 %reduce = f32[4,21760]{1,0:T(4,128)S(1)} reduce(f32[4,1,21760]{2,1,0:T(1,128)S(1)} %all-to-all-done, f32[]{:T(128)} %broadcast.99), dimensions={1}, to_apply=%all_to_all.35.reduce_sub_computation | reduce | bytes 696324 | tf_op jit(solution)/shard_map/all_to_all | solution.py:16
  19.0 2.2 %reshape.91 = f32[1280,1,2,34]{3,2,1,0:T(2,128)S(1)} reshape(f32[4,21760]{1,0:T(4,128)S(1)} %reduce) | data formatting | bytes 696320
  21.3 1.3 %copy.30 = f32[1,34,2,4,320]{4,2,1,3,0:T(2,128)S(1)} copy(f32[1,34,2,4,320]{1,2,4,3,0:T(2,128)S(1)} %bitcast.70) | data formatting | bytes 696320 | tf_op jit(solution)/shard_map/all_to_all | solution.py:16
  23.6 1.0 %copy.32 = f32[1,136,2,320]{3,2,0,1:T(2,128)} copy(f32[1,136,2,320]{3,1,2,0:T(8,128)S(1)} %convolution_bitcast_fusion) | data formatting | bytes 696320 | tf_op jit(solution)/shard_map/lk,wkcn->wlcn/transpose | solution.py:24
  24.6 3.6 %all-to-all-start.1 = ((f32[1,136,2,320]{3,2,0,1:T(2,128)}), f32[1,136,2,320]{3,2,0,1:T(2,128)S(1)}, u32[]{:S(2)}, u32[]{:S(2)}) async-start(f32[1,136,2,320]{3,2,0,1:T(2,128)} %copy.32), calls=%async_computation.1 | async-start | bytes 835584 | tf_op jit(solution)/shard_map/all_to_all | solution.py:28
  29.5 6.4 %all-to-all-done.1 = f32[1,136,2,320]{3,2,0,1:T(2,128)S(1)} async-done(((f32[1,136,2,320]{3,2,0,1:T(2,128)}), f32[1,136,2,320]{3,2,0,1:T(2,128)S(1)}, u32[]{:S(2)}, u32[]{:S(2)}) %all-to-all-start.1) | async-done | bytes 348192 | tf_op jit(solution)/shard_map/all_to_all | solution.py:28
  36.3 0.8 convolution_bitcast_fusion.2
  37.1 0.7 reshape.92
  37.8 6.5 %all-to-all-start.2 = ((f32[8,1,136]{2,1,0:T(1,128)}), f32[8,1,136]{2,1,0:T(1,128)S(1)}, u32[]{:S(2)}, u32[]{:S(2)}) async-start(f32[8,1,136]{2,1,0:T(1,128)} %reshape.92), calls=%async_computation.2 | async-start | bytes 16384 | tf_op jit(solution)/shard_map/all_to_all | solution.py:33
  44.3 6.5 %all-to-all-done.2 = f32[8,1,136]{2,1,0:T(1,128)S(1)} async-done(((f32[8,1,136]{2,1,0:T(1,128)}), f32[8,1,136]{2,1,0:T(1,128)S(1)}, u32[]{:S(2)}, u32[]{:S(2)}) %all-to-all-start.2) | async-done | bytes 4384 | tf_op jit(solution)/shard_map/all_to_all | solution.py:33
  51.6 26.6 %while.12 = (s32[]{:T(128)}, f32[2,34,5136]{2,0,1:T(2,128)S(1)}, f32[2,34,8,2]{1,2,3,0:T(8,128)S(1)}, s32[8]{0:T(128)S(1)}, s32[2]{0:T(128)S(1)}, /*index=5*/s32[]{:T(128)}, s32[]{:T(128)}) while((s32[]{:T(128)}, f32[2,34,5136]{2,0,1:T(2,128)S(1)}, f32[2,34,8,2]{1,2,3,0:T(8,128)S(1)}, s32[8]{0:T(128)S(1)}, ...), condition=%wide.region_1.2_spmd.clone.clone, body=%wide.region_0.1_spmd.clone.clone.sunk | while | flops 34329884 | bytes 4202137 | solution.py:50
  54.8 2.3 %cosine_multiply_fusion.2 = (f32[8,5136]{1,0:T(8,128)S(1)}, f32[8,5136]{1,0:T(8,128)S(1)}) fusion(f32[8]{0:T(128)S(1)} %compare_select_fusion.3, f32[]{:T(128)S(6)} %convert_element_type.54, pred[]{:T(512)S(6)} %lt.78, s32[]{:T(128)S(6)} %select_n.59, s32[8]{0:T(128)S(1)} %get-tuple-element.139), kind=kLoop, calls=%fused_computation.15.clone.1 | loop fusion | flops 534144 | bytes 328777 | tf_op jit(solution)/shard_map/while/body/eval_jaxpr/mul | solution.py:44
  57.8 0.9 %fusion.38 = f32[1,34,5136]{2,1,0:T(8,128)S(1)} fusion(f32[5136]{0:T(1024)S(1)} %fusion.37, f32[8,5136]{1,0:T(8,128)S(1)} %get-tuple-element.118, f32[8,5136]{1,0:T(8,128)S(1)} %get-tuple-element.119, f32[34,8]{0,1:T(8,128)S(1)} %get-tuple-element.120, f32[34,8]{0,1:T(8,128)S(1)} %get-tuple-element.121), kind=kOutput, calls=%fused_computation.2.clone.1 | convolution fusion | flops 33785152 | bytes 1049920 | tf_op jit(solution)/shard_map/while/body/eval_jaxpr/dot_general | solution.py:47
  58.7 0.7 copy.49
  59.4 5.3 %dynamic_update_slice.7 = f32[2,34,5136]{2,0,1:T(2,128)S(1)} dynamic-update-slice(f32[2,34,5136]{2,0,1:T(2,128)S(1)} %get-tuple-element.130, f32[1,34,5136]{2,0,1:T(1,128)S(1)} %copy.49, s32[]{:T(128)} %get-tuple-element.129, s32[]{:T(128)} %constant.25.clone.1..sunk, s32[]{:T(128)} %constant.25.clone.1..sunk) | dynamic-update-slice | bytes 1396996 | tf_op jit(solution)/shard_map/while/body/jit(dynamic_update_index_in_dim)/dynamic_update_slice | solution.py:50
  68.0 2.3 %cosine_multiply_fusion.2 = (f32[8,5136]{1,0:T(8,128)S(1)}, f32[8,5136]{1,0:T(8,128)S(1)}) fusion(f32[8]{0:T(128)S(1)} %compare_select_fusion.3, f32[]{:T(128)S(6)} %convert_element_type.54, pred[]{:T(512)S(6)} %lt.78, s32[]{:T(128)S(6)} %select_n.59, s32[8]{0:T(128)S(1)} %get-tuple-element.139), kind=kLoop, calls=%fused_computation.15.clone.1 | loop fusion | flops 534144 | bytes 328777 | tf_op jit(solution)/shard_map/while/body/eval_jaxpr/mul | solution.py:44
  71.0 0.9 %fusion.38 = f32[1,34,5136]{2,1,0:T(8,128)S(1)} fusion(f32[5136]{0:T(1024)S(1)} %fusion.37, f32[8,5136]{1,0:T(8,128)S(1)} %get-tuple-element.118, f32[8,5136]{1,0:T(8,128)S(1)} %get-tuple-element.119, f32[34,8]{0,1:T(8,128)S(1)} %get-tuple-element.120, f32[34,8]{0,1:T(8,128)S(1)} %get-tuple-element.121), kind=kOutput, calls=%fused_computation.2.clone.1 | convolution fusion | flops 33785152 | bytes 1049920 | tf_op jit(solution)/shard_map/while/body/eval_jaxpr/dot_general | solution.py:47
  71.9 0.7 copy.49
  72.6 5.5 %dynamic_update_slice.7 = f32[2,34,5136]{2,0,1:T(2,128)S(1)} dynamic-update-slice(f32[2,34,5136]{2,0,1:T(2,128)S(1)} %get-tuple-element.130, f32[1,34,5136]{2,0,1:T(1,128)S(1)} %copy.49, s32[]{:T(128)} %get-tuple-element.129, s32[]{:T(128)} %constant.25.clone.1..sunk, s32[]{:T(128)} %constant.25.clone.1..sunk) | dynamic-update-slice | bytes 1396996 | tf_op jit(solution)/shard_map/while/body/jit(dynamic_update_index_in_dim)/dynamic_update_slice | solution.py:50
  78.1 1.1 %copy-done.5 = f32[2,34,5136]{2,0,1:T(2,128)} copy-done((f32[2,34,5136]{2,0,1:T(2,128)}, f32[2,34,5136]{2,0,1:T(2,128)S(1)}, u32[]{:S(2)}) %copy-start.5) | copy-done | bytes 1397016
  (37 shorter events, 7.9 us)
Async XLA Ops:
  0.0 22.5 %copy-start = (f32[136,136]{1,0:T(8,128)S(1)}, f32[136,136]{1,0:T(8,128)}, u32[]{:S(2)}) copy-start(f32[136,136]{1,0:T(8,128)} %param.10) | copy-start | bytes 221956
  2.6 7.3 %copy-start.4 = (f32[136]{0:T(256)S(1)}, f32[136]{0:T(256)}, u32[]{:S(2)}) copy-start(f32[136]{0:T(256)} %param.12) | copy-start | bytes 1636
  5.7 11.2 %all-to-all-start = ((f32[4,1,21760]{2,1,0:T(1,128)}), f32[4,1,21760]{2,1,0:T(1,128)S(1)}, u32[]{:S(2)}, u32[]{:S(2)}) async-start(f32[4,1,21760]{2,1,0:T(1,128)} %reshape.90), calls=%async_computation | async-start | bytes 696320 | tf_op jit(solution)/shard_map/all_to_all | solution.py:16
  21.3 1.8 %copy-start.1 = (f32[136,136]{1,0:T(8,128)S(1)}, f32[136,136]{1,0:T(8,128)}, u32[]{:S(2)}) copy-start(f32[136,136]{1,0:T(8,128)} %param.11) | copy-start | bytes 221956
  23.1 5.1 %copy-start.3 = (s32[8]{0:T(128)S(1)}, s32[8]{0:T(128)}, u32[]{:S(2)}) copy-start(s32[8]{0:T(128)} %param.14) | copy-start | bytes 100
  24.6 11.7 %copy-start.2 = (f32[1,16,1280]{2,1,0:T(8,128)S(1)}, f32[1,16,1280]{2,1,0:T(8,128)}, u32[]{:S(2)}) copy-start(f32[1,16,1280]{2,1,0:T(8,128)} %param.13) | copy-start | bytes 245764
  24.6 27.0 %copy-start.6 = (s32[2]{0:T(128)S(1)}, s32[2]{0:T(128)}, u32[]{:S(2)}) copy-start(s32[2]{0:T(128)} %param.15) | copy-start | bytes 28
  24.6 11.3 %all-to-all-start.1 = ((f32[1,136,2,320]{3,2,0,1:T(2,128)}), f32[1,136,2,320]{3,2,0,1:T(2,128)S(1)}, u32[]{:S(2)}, u32[]{:S(2)}) async-start(f32[1,136,2,320]{3,2,0,1:T(2,128)} %copy.32), calls=%async_computation.1 | async-start | bytes 835584 | tf_op jit(solution)/shard_map/all_to_all | solution.py:28
  37.8 13.0 %all-to-all-start.2 = ((f32[8,1,136]{2,1,0:T(1,128)}), f32[8,1,136]{2,1,0:T(1,128)S(1)}, u32[]{:S(2)}, u32[]{:S(2)}) async-start(f32[8,1,136]{2,1,0:T(1,128)} %reshape.92), calls=%async_computation.2 | async-start | bytes 16384 | tf_op jit(solution)/shard_map/all_to_all | solution.py:33
  78.1 1.1 %copy-start.5 = (f32[2,34,5136]{2,0,1:T(2,128)}, f32[2,34,5136]{2,0,1:T(2,128)S(1)}, u32[]{:S(2)}) copy-start(f32[2,34,5136]{2,0,1:T(2,128)S(1)} %get-tuple-element.40) | copy-start | bytes 4190980
where the time goes:
time: 79.7 us; the launch traced here: 79.2 us
  local copies, waits for them, and re-layouts  27.1 us (34%)
  waiting for transfers between devices  19.7 us (25%)
  starting transfers between devices  14.3 us (18%)
  other arithmetic  10.3 us (13%)
  loops' own time  4.04 us (5%)
  matrix products  3.55 us (4%)
    dynamic_update_slice x4, local copies, waits for them, and re-layouts, on_device(): lat_rows = lax.map(one_row, (jnp.moveaxis(band_data, 3, 0), lat_points))  12.3 us
    unnamed x19, local copies, waits for them, and re-layouts  9.8 us
    all_to_all x1, waiting for transfers between devices, on_device(): lax.all_to_all(spectral, 'lev', split_axis=3, concat_axis=1, tiled=True)  6.85 us
    all_to_all x1, waiting for transfers between devices, on_device(): lax.all_to_all(fourier, 'wave', split_axis=3, concat_axis=1, tiled=True)  6.51 us
    all_to_all x1, starting transfers between devices, on_device(): lax.all_to_all(fourier, 'wave', split_axis=3, concat_axis=1, tiled=True)  6.5 us
    all_to_all x1, waiting for transfers between devices, on_device(): lax.all_to_all(divergence, 'lev', split_axis=1, concat_axis=3, tiled=True)  6.37 us
    mul x2, other arithmetic, one_row(): jnp.cos(phases) * weight[:, None]  4.69 us
    all_to_all x1, starting transfers between devices, on_device(): lax.all_to_all(spectral, 'lev', split_axis=3, concat_axis=1, tiled=True)  4.21 us
  transfers between devices with their start and end apart: 3, of which 3 were waited for; matrix products, arithmetic and copies ran while one was open for 2% of the time, Pallas kernels for 0%

commit v1 on v0

--- a/solution.py
+++ b/solution.py
@@ -13,7 +13,10 @@
     waves_here = spectral.shape[0]
     total_orders = spectral.shape[3]
     block_len = total_orders // lax.axis_size("lev")
-    columns = lax.all_to_all(spectral, "lev", split_axis=3, concat_axis=1, tiled=True)
+    columns = jnp.concatenate(
+        lax.all_to_all(jnp.stack(jnp.split(spectral, lax.axis_size("lev"), axis=3)), "lev", 0, 0),
+        axis=1,
+    )
     mode_coeffs = jnp.einsum("kl,wlcn->wkcn", to_modes, columns, precision=highest)
     first_order = lax.axis_index("lev") * block_len
     order_ids = first_order + jnp.arange(block_len)

time: 79.7 us -> 72.1 us (0.905)
  local copies, waits for them, and re-layouts: 27.1 us -> 19.3 us
  waiting for transfers between devices: 19.7 us -> 20.5 us
    unnamed x19 -> x16, local copies, waits for them, and re-layouts: 9.8 us -> 1.89 us
    all_to_all x2 -> x0, local copies, waits for them, and re-layouts: 1.79 us -> none  [on_device(): lax.all_to_all(spectral, 'lev', split_axis=3, concat_axis=1, tiled=True)]
    all_to_all x1 -> x0, other arithmetic: 1.62 us -> none  [on_device(): lax.all_to_all(spectral, 'lev', split_axis=3, concat_axis=1, tiled=True)]
    another operation x2 -> x3, local copies, waits for them, and re-layouts: 0.4 us -> 1.79 us  [the longest x1 1.4 us: on_device(): jnp.stack(jnp.split(spectral, lax.axis_size('lev'), axis=3))]
    another operation x0 -> x1, other arithmetic: none -> 0.95 us  [on_device(): jnp.stack(jnp.split(spectral, lax.axis_size('lev'), axis=3))]
where the time goes in v1:
time: 72.1 us; the launch traced here: 71.6 us
  waiting for transfers between devices  20.5 us (28%)
  local copies, waits for them, and re-layouts  19.3 us (27%)
  starting transfers between devices  14.4 us (20%)
  other arithmetic  9.65 us (13%)
  loops' own time  4.04 us (6%)
  matrix products  3.55 us (5%)
    dynamic_update_slice x4, local copies, waits for them, and re-layouts, on_device(): lat_rows = lax.map(one_row, (jnp.moveaxis(band_data, 3, 0), lat_points))  12.3 us
    all_to_all x1, waiting for transfers between devices, on_device(): lax.all_to_all(jnp.stack(jnp.split(spectral, lax.axis_size('lev'), axis=3...  7.6 us
    all_to_all x1, waiting for transfers between devices, on_device(): lax.all_to_all(fourier, 'wave', split_axis=3, concat_axis=1, tiled=True)  6.51 us
    all_to_all x1, starting transfers between devices, on_device(): lax.all_to_all(fourier, 'wave', split_axis=3, concat_axis=1, tiled=True)  6.51 us
    all_to_all x1, waiting for transfers between devices, on_device(): lax.all_to_all(divergence, 'lev', split_axis=1, concat_axis=3, tiled=True)  6.4 us
    mul x2, other arithmetic, one_row(): jnp.cos(phases) * weight[:, None]  4.69 us
    all_to_all x1, starting transfers between devices, on_device(): lax.all_to_all(jnp.stack(jnp.split(spectral, lax.axis_size('lev'), axis=3...  4.34 us
    another operation x1, loops' own time, on_device(): lat_rows = lax.map(one_row, (jnp.moveaxis(band_data, 3, 0), lat_points))  4.04 us
  transfers between devices with their start and end apart: 3, of which 3 were waited for; matrix products, arithmetic and copies ran while one was open for 2% of the time, Pallas kernels for 0%

profile of v1, /device:TPU:0, one launch (start us, length us, event | category | flops | bytes accessed | tf_op | source)
XLA Modules:
  0.0 71.6 jit_solution(1712684438005486869)
XLA Ops:
  0.0 1.4 %slice_bitcast_fusion.4 = (f32[1,1,34,2,320]{4,3,2,1,0:T(2,128)S(1)}, f32[1,1,34,2,320]{4,3,2,1,0:T(2,128)S(1)}, f32[1,1,34,2,320]{4,3,2,1,0:T(2,128)S(1)}, f32[1,1,34,2,320]{4,3,2,1,0:T(2,128)S(1)}) fusion(f32[1,34,2,1280]{3,2,1,0:T(2,128)} %param.9), kind=kLoop, calls=%fused_computation.43 | loop fusion | bytes 696320 | tf_op jit(solution)/shard_map/stack | solution.py:17
  1.4 1.0 %pad_maximum_fusion = f32[4,1,34,2,320]{4,3,2,1,0:T(2,128)} fusion(f32[1,1,34,2,320]{4,3,2,1,0:T(2,128)S(1)} %get-tuple-element.85, f32[1,1,34,2,320]{4,3,2,1,0:T(2,128)S(1)} %get-tuple-element.86, f32[1,1,34,2,320]{4,3,2,1,0:T(2,128)S(1)} %get-tuple-element.84, f32[1,1,34,2,320]{4,3,2,1,0:T(2,128)S(1)} %get-tuple-element.83), kind=kLoop, calls=%fused_computation.35 | loop fusion | flops 261120 | bytes 696320 | tf_op jit(solution)/shard_map/stack | solution.py:17
  2.4 4.3 %all-to-all-start = ((f32[4,1,34,2,320]{4,3,2,1,0:T(2,128)}), f32[4,1,34,2,320]{4,3,2,1,0:T(2,128)S(1)}, u32[]{:S(2)}, u32[]{:S(2)}) async-start(f32[4,1,34,2,320]{4,3,2,1,0:T(2,128)} %pad_maximum_fusion), calls=%async_computation | async-start | bytes 835584 | tf_op jit(solution)/shard_map/all_to_all | solution.py:17
  6.8 7.6 %all-to-all-done = f32[4,1,34,2,320]{4,3,2,1,0:T(2,128)S(1)} async-done(((f32[4,1,34,2,320]{4,3,2,1,0:T(2,128)}), f32[4,1,34,2,320]{4,3,2,1,0:T(2,128)S(1)}, u32[]{:S(2)}, u32[]{:S(2)}) %all-to-all-start) | async-done | bytes 348192 | tf_op jit(solution)/shard_map/all_to_all | solution.py:17
  15.5 1.0 %copy.20 = f32[1,136,2,320]{3,2,0,1:T(2,128)} copy(f32[1,136,2,320]{3,1,2,0:T(8,128)S(1)} %convolution_bitcast_fusion) | data formatting | bytes 696320 | tf_op jit(solution)/shard_map/lk,wkcn->wlcn/transpose | solution.py:27
  16.5 3.6 %all-to-all-start.1 = ((f32[1,136,2,320]{3,2,0,1:T(2,128)}), f32[1,136,2,320]{3,2,0,1:T(2,128)S(1)}, u32[]{:S(2)}, u32[]{:S(2)}) async-start(f32[1,136,2,320]{3,2,0,1:T(2,128)} %copy.20), calls=%async_computation.1 | async-start | bytes 835584 | tf_op jit(solution)/shard_map/all_to_all | solution.py:31
  21.3 6.4 %all-to-all-done.1 = f32[1,136,2,320]{3,2,0,1:T(2,128)S(1)} async-done(((f32[1,136,2,320]{3,2,0,1:T(2,128)}), f32[1,136,2,320]{3,2,0,1:T(2,128)S(1)}, u32[]{:S(2)}, u32[]{:S(2)}) %all-to-all-start.1) | async-done | bytes 348192 | tf_op jit(solution)/shard_map/all_to_all | solution.py:31
  28.1 0.8 %convolution_bitcast_fusion.2 = f32[34,1,2,16]{0,3,2,1:T(8,128)S(1)} fusion(f32[34,2,1280]{2,0,1:T(8,128)S(1)} %reshape.90, f32[1,16,1280]{2,1,0:T(8,128)S(1)} %copy-done.2, f32[1280]{0:T(1024)S(1)} %fusion.28), kind=kOutput, calls=%fused_computation.32 | convolution fusion | flops 16732160 | bytes 439552 | tf_op jit(solution)/shard_map/wjn,wlcn->lwcj/dot_general | solution.py:33
  29.0 0.7 reshape.91
  29.6 6.5 %all-to-all-start.2 = ((f32[8,1,136]{2,1,0:T(1,128)}), f32[8,1,136]{2,1,0:T(1,128)S(1)}, u32[]{:S(2)}, u32[]{:S(2)}) async-start(f32[8,1,136]{2,1,0:T(1,128)} %reshape.91), calls=%async_computation.2 | async-start | bytes 16384 | tf_op jit(solution)/shard_map/all_to_all | solution.py:36
  36.2 6.5 %all-to-all-done.2 = f32[8,1,136]{2,1,0:T(1,128)S(1)} async-done(((f32[8,1,136]{2,1,0:T(1,128)}), f32[8,1,136]{2,1,0:T(1,128)S(1)}, u32[]{:S(2)}, u32[]{:S(2)}) %all-to-all-start.2) | async-done | bytes 4384 | tf_op jit(solution)/shard_map/all_to_all | solution.py:36
  43.2 0.7 reduce
  44.0 26.6 %while.12 = (s32[]{:T(128)}, f32[2,34,5136]{2,0,1:T(2,128)S(1)}, f32[2,34,8,2]{1,2,3,0:T(8,128)S(1)}, s32[8]{0:T(128)S(1)}, s32[2]{0:T(128)S(1)}, /*index=5*/s32[]{:T(128)}, s32[]{:T(128)}) while((s32[]{:T(128)}, f32[2,34,5136]{2,0,1:T(2,128)S(1)}, f32[2,34,8,2]{1,2,3,0:T(8,128)S(1)}, s32[8]{0:T(128)S(1)}, ...), condition=%wide.region_1.2_spmd.clone.clone, body=%wide.region_0.1_spmd.clone.clone.sunk | while | flops 34329884 | bytes 4202137 | solution.py:53
  47.2 2.3 %cosine_multiply_fusion.2 = (f32[8,5136]{1,0:T(8,128)S(1)}, f32[8,5136]{1,0:T(8,128)S(1)}) fusion(f32[8]{0:T(128)S(1)} %compare_select_fusion.3, f32[]{:T(128)S(6)} %convert_element_type.54, pred[]{:T(512)S(6)} %lt.78, s32[]{:T(128)S(6)} %select_n.59, s32[8]{0:T(128)S(1)} %get-tuple-element.143), kind=kLoop, calls=%fused_computation.15.clone.1 | loop fusion | flops 534144 | bytes 328777 | tf_op jit(solution)/shard_map/while/body/eval_jaxpr/mul | solution.py:47
  49.5 0.7 fusion.37
  50.2 0.9 %fusion.38 = f32[1,34,5136]{2,1,0:T(8,128)S(1)} fusion(f32[5136]{0:T(1024)S(1)} %fusion.37, f32[8,5136]{1,0:T(8,128)S(1)} %get-tuple-element.122, f32[8,5136]{1,0:T(8,128)S(1)} %get-tuple-element.123, f32[34,8]{0,1:T(8,128)S(1)} %get-tuple-element.124, f32[34,8]{0,1:T(8,128)S(1)} %get-tuple-element.125), kind=kOutput, calls=%fused_computation.2.clone.1 | convolution fusion | flops 33785152 | bytes 1049920 | tf_op jit(solution)/shard_map/while/body/eval_jaxpr/dot_general | solution.py:50
  51.1 0.7 %copy.37 = f32[1,34,5136]{2,0,1:T(1,128)S(1)} copy(f32[1,34,5136]{2,1,0:T(8,128)S(1)} %fusion.38) | data formatting | bytes 1396992 | tf_op jit(solution)/shard_map/while/body/jit(dynamic_update_index_in_dim)/dynamic_update_slice | solution.py:53
  51.8 5.3 %dynamic_update_slice.7 = f32[2,34,5136]{2,0,1:T(2,128)S(1)} dynamic-update-slice(f32[2,34,5136]{2,0,1:T(2,128)S(1)} %get-tuple-element.134, f32[1,34,5136]{2,0,1:T(1,128)S(1)} %copy.37, s32[]{:T(128)} %get-tuple-element.133, s32[]{:T(128)} %constant.25.clone.1..sunk, s32[]{:T(128)} %constant.25.clone.1..sunk) | dynamic-update-slice | bytes 1396996 | tf_op jit(solution)/shard_map/while/body/jit(dynamic_update_index_in_dim)/dynamic_update_slice | solution.py:53
  60.4 2.3 %cosine_multiply_fusion.2 = (f32[8,5136]{1,0:T(8,128)S(1)}, f32[8,5136]{1,0:T(8,128)S(1)}) fusion(f32[8]{0:T(128)S(1)} %compare_select_fusion.3, f32[]{:T(128)S(6)} %convert_element_type.54, pred[]{:T(512)S(6)} %lt.78, s32[]{:T(128)S(6)} %select_n.59, s32[8]{0:T(128)S(1)} %get-tuple-element.143), kind=kLoop, calls=%fused_computation.15.clone.1 | loop fusion | flops 534144 | bytes 328777 | tf_op jit(solution)/shard_map/while/body/eval_jaxpr/mul | solution.py:47
  62.7 0.7 fusion.37
  63.4 0.9 %fusion.38 = f32[1,34,5136]{2,1,0:T(8,128)S(1)} fusion(f32[5136]{0:T(1024)S(1)} %fusion.37, f32[8,5136]{1,0:T(8,128)S(1)} %get-tuple-element.122, f32[8,5136]{1,0:T(8,128)S(1)} %get-tuple-element.123, f32[34,8]{0,1:T(8,128)S(1)} %get-tuple-element.124, f32[34,8]{0,1:T(8,128)S(1)} %get-tuple-element.125), kind=kOutput, calls=%fused_computation.2.clone.1 | convolution fusion | flops 33785152 | bytes 1049920 | tf_op jit(solution)/shard_map/while/body/eval_jaxpr/dot_general | solution.py:50
  64.3 0.7 %copy.37 = f32[1,34,5136]{2,0,1:T(1,128)S(1)} copy(f32[1,34,5136]{2,1,0:T(8,128)S(1)} %fusion.38) | data formatting | bytes 1396992 | tf_op jit(solution)/shard_map/while/body/jit(dynamic_update_index_in_dim)/dynamic_update_slice | solution.py:53
  65.0 5.5 %dynamic_update_slice.7 = f32[2,34,5136]{2,0,1:T(2,128)S(1)} dynamic-update-slice(f32[2,34,5136]{2,0,1:T(2,128)S(1)} %get-tuple-element.134, f32[1,34,5136]{2,0,1:T(1,128)S(1)} %copy.37, s32[]{:T(128)} %get-tuple-element.133, s32[]{:T(128)} %constant.25.clone.1..sunk, s32[]{:T(128)} %constant.25.clone.1..sunk) | dynamic-update-slice | bytes 1396996 | tf_op jit(solution)/shard_map/while/body/jit(dynamic_update_index_in_dim)/dynamic_update_slice | solution.py:53
  70.5 1.1 %copy-done.5 = f32[2,34,5136]{2,0,1:T(2,128)} copy-done((f32[2,34,5136]{2,0,1:T(2,128)}, f32[2,34,5136]{2,0,1:T(2,128)S(1)}, u32[]{:S(2)}) %copy-start.5) | copy-done | bytes 1397016
  (34 shorter events, 5.9 us)
Async XLA Ops:
  0.0 14.4 %copy-start = (f32[136,136]{1,0:T(8,128)S(1)}, f32[136,136]{1,0:T(8,128)}, u32[]{:S(2)}) copy-start(f32[136,136]{1,0:T(8,128)} %param.10) | copy-start | bytes 221956
  0.0 6.7 %copy-start.4 = (f32[136]{0:T(256)S(1)}, f32[136]{0:T(256)}, u32[]{:S(2)}) copy-start(f32[136]{0:T(256)} %param.12) | copy-start | bytes 1636
  2.4 12.6 %copy-start.1 = (f32[136,136]{1,0:T(8,128)S(1)}, f32[136,136]{1,0:T(8,128)}, u32[]{:S(2)}) copy-start(f32[136,136]{1,0:T(8,128)} %param.11) | copy-start | bytes 221956
  2.4 12.0 %all-to-all-start = ((f32[4,1,34,2,320]{4,3,2,1,0:T(2,128)}), f32[4,1,34,2,320]{4,3,2,1,0:T(2,128)S(1)}, u32[]{:S(2)}, u32[]{:S(2)}) async-start(f32[4,1,34,2,320]{4,3,2,1,0:T(2,128)} %pad_maximum_fusion), calls=%async_computation | async-start | bytes 835584 | tf_op jit(solution)/shard_map/all_to_all | solution.py:17
  15.0 5.1 %copy-start.3 = (s32[8]{0:T(128)S(1)}, s32[8]{0:T(128)}, u32[]{:S(2)}) copy-start(s32[8]{0:T(128)} %param.14) | copy-start | bytes 100
  16.5 11.7 %copy-start.2 = (f32[1,16,1280]{2,1,0:T(8,128)S(1)}, f32[1,16,1280]{2,1,0:T(8,128)}, u32[]{:S(2)}) copy-start(f32[1,16,1280]{2,1,0:T(8,128)} %param.13) | copy-start | bytes 245764
  16.5 27.5 %copy-start.6 = (s32[2]{0:T(128)S(1)}, s32[2]{0:T(128)}, u32[]{:S(2)}) copy-start(s32[2]{0:T(128)} %param.15) | copy-start | bytes 28
  16.5 11.3 %all-to-all-start.1 = ((f32[1,136,2,320]{3,2,0,1:T(2,128)}), f32[1,136,2,320]{3,2,0,1:T(2,128)S(1)}, u32[]{:S(2)}, u32[]{:S(2)}) async-start(f32[1,136,2,320]{3,2,0,1:T(2,128)} %copy.20), calls=%async_computation.1 | async-start | bytes 835584 | tf_op jit(solution)/shard_map/all_to_all | solution.py:31
  29.6 13.0 %all-to-all-start.2 = ((f32[8,1,136]{2,1,0:T(1,128)}), f32[8,1,136]{2,1,0:T(1,128)S(1)}, u32[]{:S(2)}, u32[]{:S(2)}) async-start(f32[8,1,136]{2,1,0:T(1,128)} %reshape.91), calls=%async_computation.2 | async-start | bytes 16384 | tf_op jit(solution)/shard_map/all_to_all | solution.py:36
  70.5 1.1 %copy-start.5 = (f32[2,34,5136]{2,0,1:T(2,128)}, f32[2,34,5136]{2,0,1:T(2,128)S(1)}, u32[]{:S(2)}) copy-start(f32[2,34,5136]{2,0,1:T(2,128)S(1)} %get-tuple-element.40) | copy-start | bytes 4190980
